TPU v7x, 32 devices: a whole 2x2x4 slice. The times are simulated.
32 devices in a mesh: srv: 8 (over y, x, core), head: 4 (over z).
Axes of the slice: x: 2, y: 2, z: 4, core: 2. Of those that a mesh axis runs over, the one named last changes fastest.
Arguments:
- queries: bfloat16 [2048, 8192], P('srv', 'head'), may hold values from -200 to 200
- key_value_pair: bfloat16 [2, 2048, 1024], P(None, 'srv', 'head'), may hold values from -200 to 200
- lengths: int32 [8], replicated, may hold values from 1 to 1024, 2048 in all
Outputs:
- attended: bfloat16 [2048, 8192], P(('srv', 'head'))
All inputs are finite; a program needn't handle non-finite values.
Results may differ from a plain program's by a relative error of at most 0.012.
Values may be sent and summed in bfloat16 or wider, within the bound.
A program may use at most 64 MiB of HBM per device.

v0:
```python
import math

import jax
import jax.numpy as jnp
from jax import lax
from jax.sharding import PartitionSpec as P

HEAD_SIZE = 128


def doc_start(doc_lengths, row_ids):
    doc_ends = jnp.cumsum(doc_lengths)
    passed = doc_ends[None, :] <= row_ids[:, None]
    return jnp.max(jnp.where(passed, doc_ends[None, :], 0), axis=1)


def apply_rotary(vectors, positions):
    half_width = vectors.shape[-1] // 2
    steps_up = jnp.arange(half_width, dtype=jnp.float32) * (2.0 / vectors.shape[-1])
    inverse = jnp.exp(-steps_up * math.log(500000.0))
    angles = positions[:, None] * inverse[None, :]
    cosine = jnp.cos(angles)[:, None, :]
    sine_table = jnp.sin(angles)[:, None, :]
    low_half = vectors[..., :half_width]
    high_half = vectors[..., half_width:]
    return jnp.concatenate(
        [low_half * cosine - high_half * sine_table, high_half * cosine + low_half * sine_table],
        axis=-1,
    )


def merge_shard(state, query_group, row_group, start_group, key_rows, value_rows, key_ids):
    run_max, run_total, run_acc = state
    group_rows, kv_local, per_kv, head_width = query_group.shape
    all_heads = kv_local * per_kv
    scores = jnp.einsum(
        "rhgd,khd->hgrk", query_group, key_rows, preferred_element_type=jnp.float32
    ) * HEAD_SIZE ** (-0.5)
    allowed = (
        (key_ids[None, :] <= row_group[:, None]) & (key_ids[None, :] >= start_group[:, None])
    )[None, None]
    masked = jnp.where(allowed, scores, -1e30)
    shard_max = jnp.max(masked, axis=3)
    weights = jnp.where(allowed, jnp.exp(masked - shard_max[..., None]), 0.0)
    shard_total = jnp.sum(weights, axis=3)
    part_value = jnp.einsum(
        "hgrk,khd->rhgd",
        weights.astype(jnp.bfloat16),
        value_rows,
        preferred_element_type=jnp.float32,
    ).reshape(group_rows, all_heads, head_width)
    shard_max = jnp.transpose(shard_max, (2, 0, 1)).reshape(group_rows, all_heads)
    shard_total = jnp.transpose(shard_total, (2, 0, 1)).reshape(group_rows, all_heads)
    new_max = jnp.maximum(run_max, shard_max)
    old_factor = jnp.exp(run_max - new_max)
    new_factor = jnp.exp(shard_max - new_max)
    new_total = run_total * old_factor + shard_total * new_factor
    new_acc = run_acc * old_factor[..., None] + part_value * new_factor[..., None]
    return (new_max, new_total, new_acc)


def attend(query_flat, row_ids, starts, packed_pair, shard_rows, kv_local):
    total_rows, query_width = query_flat.shape
    all_heads = query_width // HEAD_SIZE
    per_kv = all_heads // kv_local
    group_rows = min(total_rows, 64)
    group_count = total_rows // group_rows
    query_view = query_flat.reshape(total_rows, kv_local, per_kv, HEAD_SIZE)

    def add_shard(state, kv_shard, key_low):
        kv_view = kv_shard.reshape(shard_rows, 2, kv_local, HEAD_SIZE)
        key_rows = kv_view[:, 0]
        value_rows = kv_view[:, 1]
        key_ids = key_low + jnp.arange(shard_rows, dtype=jnp.int32)
        key_high = key_low + shard_rows - 1
        updated = []
        for group_index in range(group_count):
            row_slice = slice(group_index * group_rows, (group_index + 1) * group_rows)
            group_state = (state[0][row_slice], state[1][row_slice], state[2][row_slice])
            needed = jnp.any((starts[row_slice] <= key_high) & (row_ids[row_slice] >= key_low))
            group_state = lax.cond(
                needed,
                lambda current, row_slice=row_slice: merge_shard(
                    current,
                    query_view[row_slice],
                    row_ids[row_slice],
                    starts[row_slice],
                    key_rows,
                    value_rows,
                    key_ids,
                ),
                lambda current: current,
                group_state,
            )
            updated.append(group_state)
        return (
            jnp.concatenate([item[0] for item in updated], axis=0),
            jnp.concatenate([item[1] for item in updated], axis=0),
            jnp.concatenate([item[2] for item in updated], axis=0),
        )

    initial = (
        jnp.full((total_rows, all_heads), -1e30, jnp.float32),
        jnp.zeros((total_rows, all_heads), jnp.float32),
        jnp.zeros((total_rows, all_heads, HEAD_SIZE), jnp.float32),
    )
    running = initial
    kv_piece = lax.all_gather(packed_pair, "srv", axis=0, tiled=True)
    shard_count = kv_piece.shape[0] // shard_rows
    shards = kv_piece.reshape(shard_count, shard_rows, kv_piece.shape[1])

    def one_step(current, packed):
        kv_shard, shard_index = packed
        return (add_shard(current, kv_shard, shard_index * shard_rows), None)

    running, _ = lax.scan(one_step, running, (shards, jnp.arange(shard_count, dtype=jnp.int32)))
    run_max, run_total, run_acc = running
    return (run_acc / run_total[..., None]).reshape(total_rows, query_width).astype(jnp.bfloat16)


def body(queries, key_value_pair, lengths):
    tok_rows = queries.shape[0]
    query_width = queries.shape[1]
    all_heads = query_width // HEAD_SIZE
    kv_local = key_value_pair.shape[2] // HEAD_SIZE
    own_index = lax.axis_index("srv")
    local_ids = jnp.arange(tok_rows, dtype=jnp.int32)
    row_ids = own_index * tok_rows + local_ids
    starts = doc_start(lengths, row_ids)
    positions = (row_ids - starts).astype(jnp.float32)
    query_rotated = apply_rotary(
        queries.reshape(tok_rows, all_heads, HEAD_SIZE).astype(jnp.float32), positions
    ).astype(jnp.bfloat16)
    key_rotated = apply_rotary(
        key_value_pair[0].reshape(tok_rows, kv_local, HEAD_SIZE).astype(jnp.float32), positions
    ).astype(jnp.bfloat16)
    packed_pair = jnp.stack(
        [key_rotated, key_value_pair[1].reshape(tok_rows, kv_local, HEAD_SIZE)], axis=1
    )
    packed_pair = packed_pair.reshape(tok_rows, 2 * kv_local * HEAD_SIZE)
    query_flat = query_rotated.reshape(tok_rows, query_width)
    result = attend(query_flat, row_ids, starts, packed_pair, tok_rows, kv_local)
    return lax.all_to_all(result, "head", split_axis=0, concat_axis=1, tiled=True)


def solution(mesh):
    in_specs = (P("srv", "head"), P(None, "srv", "head"), P())
    out_specs = P(("srv", "head"), None)
    return jax.shard_map(body, mesh=mesh, in_specs=in_specs, out_specs=out_specs, check_vma=False)
```

profile of v0, /device:TPU:6, one launch (start us, length us, event | category | flops | bytes accessed | tf_op | source)
XLA Modules:
  0.0 176.5 jit_solution(17758708910333524287)
XLA Ops:
  13.4 25.0 %all-gather.2.cloned.1.call-done = bf16[2048,512]{0,1:T(8,128)(2,1)} async-done(((bf16[256,512]{0,1:T(8,128)(2,1)}), bf16[2048,512]{0,1:T(8,128)(2,1)}) %all-gather.2.cloned.1.call-update) | async-done | bytes 2097168 | tf_op jit(solution)/shard_map/all_gather | solution.py:108
  38.4 3.9 %copy.46 = bf16[2048,512]{1,0:T(8,128)(2,1)} copy(bf16[2048,512]{0,1:T(8,128)(2,1)} %all-gather.2.cloned.1.call-done) | data formatting | bytes 4194304 | tf_op jit(solution)/shard_map/all_gather | solution.py:108
  42.4 1.5 broadcast_in_dim.125
  43.9 101.3 %while.18 = (s32[]{:T(128)}, f32[256,16]{0,1:T(8,128)S(1)}, f32[256,16]{0,1:T(8,128)S(1)}, f32[256,16,128]{2,0,1:T(8,128)}, s32[256]{0:T(256)S(1)}, /*index=5*/s...) while((s32[]{:T(128)}, f32[256,16]{0,1:T(8,128)S(1)}, ...), condition=%wide.region_23.24_spmd, body=%wide.region_2.23_spmd.sunk | while | flops 549692672 | bytes 33666752 | solution.py:116
  46.4 1.7 fusion.81
  55.3 1.7 fusion.81
  64.2 1.7 fusion.81
  69.1 1.4 pad_maximum_fusion.10
  73.1 1.7 fusion.81
  76.2 1.8 %conditional.11 = ((f32[64,16]{0,1:T(8,128)S(1)}, f32[64,16]{0,1:T(8,128)S(1)}, f32[64,16,128]{2,0,1:T(8,128)S(1)})) conditional(s32[]{:T(128)} %convert_element_type.112, (f32[64,16]{0,1:T(8,128)S(1)}, f32[64,16]{0,1:T(8,128)S(1)}, f32[64,16,128]{2,0,1:T(8,128)S(1)}) %tuple.136, (s32[256]{0:T(256)S(1)}, s32[256]{0:T(256)S(1)}, s32[256]{0:T(256)S(1)}, ...), branch_computations={%region_4.4_spmd, %region_5.7_spmd} | conditional | flops 137023488 | bytes 5892640 | solution.py:81
  78.6 1.9 %conditional.10 = ((f32[64,16]{0,1:T(8,128)S(1)}, f32[64,16]{0,1:T(8,128)S(1)}, f32[64,16,128]{2,0,1:T(8,128)S(1)})) conditional(s32[]{:T(128)} %convert_element_type.111, (f32[64,16]{0,1:T(8,128)S(1)}, f32[64,16]{0,1:T(8,128)S(1)}, f32[64,16,128]{2,0,1:T(8,128)S(1)}) %tuple.134, (s32[256]{0:T(256)S(1)}, s32[256]{0:T(256)S(1)}, s32[256]{0:T(256)S(1)}, ...), branch_computations={%region_9.9_spmd, %region_10.12_spmd} | conditional | flops 137023488 | bytes 5892640 | solution.py:81
  81.1 1.8 %conditional.9 = ((f32[64,16]{0,1:T(8,128)S(1)}, f32[64,16]{0,1:T(8,128)S(1)}, f32[64,16,128]{2,0,1:T(8,128)S(1)})) conditional(s32[]{:T(128)} %convert_element_type.110, (f32[64,16]{0,1:T(8,128)S(1)}, f32[64,16]{0,1:T(8,128)S(1)}, f32[64,16,128]{2,0,1:T(8,128)S(1)}) %tuple.132, (s32[256]{0:T(256)S(1)}, s32[256]{0:T(256)S(1)}, s32[256]{0:T(256)S(1)}, ...), branch_computations={%region_14.14_spmd, %region_15.17_spmd} | conditional | flops 137023488 | bytes 5892640 | solution.py:81
  83.6 1.9 %conditional.8 = ((f32[64,16]{0,1:T(8,128)S(1)}, f32[64,16]{0,1:T(8,128)S(1)}, f32[64,16,128]{2,0,1:T(8,128)S(1)})) conditional(s32[]{:T(128)} %convert_element_type.109, (f32[64,16]{0,1:T(8,128)S(1)}, f32[64,16]{0,1:T(8,128)S(1)}, f32[64,16,128]{2,0,1:T(8,128)S(1)}) %tuple.130, (s32[256]{0:T(256)S(1)}, s32[256]{0:T(256)S(1)}, s32[256]{0:T(256)S(1)}, ...), branch_computations={%region_19.19_spmd, %region_20.22_spmd} | conditional | flops 137023488 | bytes 5892640 | solution.py:81
  89.6 1.7 fusion.81
  92.6 1.8 %conditional.11 = ((f32[64,16]{0,1:T(8,128)S(1)}, f32[64,16]{0,1:T(8,128)S(1)}, f32[64,16,128]{2,0,1:T(8,128)S(1)})) conditional(s32[]{:T(128)} %convert_element_type.112, (f32[64,16]{0,1:T(8,128)S(1)}, f32[64,16]{0,1:T(8,128)S(1)}, f32[64,16,128]{2,0,1:T(8,128)S(1)}) %tuple.136, (s32[256]{0:T(256)S(1)}, s32[256]{0:T(256)S(1)}, s32[256]{0:T(256)S(1)}, ...), branch_computations={%region_4.4_spmd, %region_5.7_spmd} | conditional | flops 137023488 | bytes 5892640 | solution.py:81
  95.0 1.9 %conditional.10 = ((f32[64,16]{0,1:T(8,128)S(1)}, f32[64,16]{0,1:T(8,128)S(1)}, f32[64,16,128]{2,0,1:T(8,128)S(1)})) conditional(s32[]{:T(128)} %convert_element_type.111, (f32[64,16]{0,1:T(8,128)S(1)}, f32[64,16]{0,1:T(8,128)S(1)}, f32[64,16,128]{2,0,1:T(8,128)S(1)}) %tuple.134, (s32[256]{0:T(256)S(1)}, s32[256]{0:T(256)S(1)}, s32[256]{0:T(256)S(1)}, ...), branch_computations={%region_9.9_spmd, %region_10.12_spmd} | conditional | flops 137023488 | bytes 5892640 | solution.py:81
  97.5 1.8 %conditional.9 = ((f32[64,16]{0,1:T(8,128)S(1)}, f32[64,16]{0,1:T(8,128)S(1)}, f32[64,16,128]{2,0,1:T(8,128)S(1)})) conditional(s32[]{:T(128)} %convert_element_type.110, (f32[64,16]{0,1:T(8,128)S(1)}, f32[64,16]{0,1:T(8,128)S(1)}, f32[64,16,128]{2,0,1:T(8,128)S(1)}) %tuple.132, (s32[256]{0:T(256)S(1)}, s32[256]{0:T(256)S(1)}, s32[256]{0:T(256)S(1)}, ...), branch_computations={%region_14.14_spmd, %region_15.17_spmd} | conditional | flops 137023488 | bytes 5892640 | solution.py:81
  99.9 1.9 %conditional.8 = ((f32[64,16]{0,1:T(8,128)S(1)}, f32[64,16]{0,1:T(8,128)S(1)}, f32[64,16,128]{2,0,1:T(8,128)S(1)})) conditional(s32[]{:T(128)} %convert_element_type.109, (f32[64,16]{0,1:T(8,128)S(1)}, f32[64,16]{0,1:T(8,128)S(1)}, f32[64,16,128]{2,0,1:T(8,128)S(1)}) %tuple.130, (s32[256]{0:T(256)S(1)}, s32[256]{0:T(256)S(1)}, s32[256]{0:T(256)S(1)}, ...), branch_computations={%region_19.19_spmd, %region_20.22_spmd} | conditional | flops 137023488 | bytes 5892640 | solution.py:81
  101.9 1.4 pad_maximum_fusion.10
  105.9 1.7 fusion.81
  109.0 1.8 %conditional.11 = ((f32[64,16]{0,1:T(8,128)S(1)}, f32[64,16]{0,1:T(8,128)S(1)}, f32[64,16,128]{2,0,1:T(8,128)S(1)})) conditional(s32[]{:T(128)} %convert_element_type.112, (f32[64,16]{0,1:T(8,128)S(1)}, f32[64,16]{0,1:T(8,128)S(1)}, f32[64,16,128]{2,0,1:T(8,128)S(1)}) %tuple.136, (s32[256]{0:T(256)S(1)}, s32[256]{0:T(256)S(1)}, s32[256]{0:T(256)S(1)}, ...), branch_computations={%region_4.4_spmd, %region_5.7_spmd} | conditional | flops 137023488 | bytes 5892640 | solution.py:81
  111.4 1.9 %conditional.10 = ((f32[64,16]{0,1:T(8,128)S(1)}, f32[64,16]{0,1:T(8,128)S(1)}, f32[64,16,128]{2,0,1:T(8,128)S(1)})) conditional(s32[]{:T(128)} %convert_element_type.111, (f32[64,16]{0,1:T(8,128)S(1)}, f32[64,16]{0,1:T(8,128)S(1)}, f32[64,16,128]{2,0,1:T(8,128)S(1)}) %tuple.134, (s32[256]{0:T(256)S(1)}, s32[256]{0:T(256)S(1)}, s32[256]{0:T(256)S(1)}, ...), branch_computations={%region_9.9_spmd, %region_10.12_spmd} | conditional | flops 137023488 | bytes 5892640 | solution.py:81
  113.9 1.8 %conditional.9 = ((f32[64,16]{0,1:T(8,128)S(1)}, f32[64,16]{0,1:T(8,128)S(1)}, f32[64,16,128]{2,0,1:T(8,128)S(1)})) conditional(s32[]{:T(128)} %convert_element_type.110, (f32[64,16]{0,1:T(8,128)S(1)}, f32[64,16]{0,1:T(8,128)S(1)}, f32[64,16,128]{2,0,1:T(8,128)S(1)}) %tuple.132, (s32[256]{0:T(256)S(1)}, s32[256]{0:T(256)S(1)}, s32[256]{0:T(256)S(1)}, ...), branch_computations={%region_14.14_spmd, %region_15.17_spmd} | conditional | flops 137023488 | bytes 5892640 | solution.py:81
  116.4 1.9 %conditional.8 = ((f32[64,16]{0,1:T(8,128)S(1)}, f32[64,16]{0,1:T(8,128)S(1)}, f32[64,16,128]{2,0,1:T(8,128)S(1)})) conditional(s32[]{:T(128)} %convert_element_type.109, (f32[64,16]{0,1:T(8,128)S(1)}, f32[64,16]{0,1:T(8,128)S(1)}, f32[64,16,128]{2,0,1:T(8,128)S(1)}) %tuple.130, (s32[256]{0:T(256)S(1)}, s32[256]{0:T(256)S(1)}, s32[256]{0:T(256)S(1)}, ...), branch_computations={%region_19.19_spmd, %region_20.22_spmd} | conditional | flops 137023488 | bytes 5892640 | solution.py:81
  122.4 1.7 fusion.81
  125.4 1.8 %conditional.11 = ((f32[64,16]{0,1:T(8,128)S(1)}, f32[64,16]{0,1:T(8,128)S(1)}, f32[64,16,128]{2,0,1:T(8,128)S(1)})) conditional(s32[]{:T(128)} %convert_element_type.112, (f32[64,16]{0,1:T(8,128)S(1)}, f32[64,16]{0,1:T(8,128)S(1)}, f32[64,16,128]{2,0,1:T(8,128)S(1)}) %tuple.136, (s32[256]{0:T(256)S(1)}, s32[256]{0:T(256)S(1)}, s32[256]{0:T(256)S(1)}, ...), branch_computations={%region_4.4_spmd, %region_5.7_spmd} | conditional | flops 137023488 | bytes 5892640 | solution.py:81
  127.8 1.9 %conditional.10 = ((f32[64,16]{0,1:T(8,128)S(1)}, f32[64,16]{0,1:T(8,128)S(1)}, f32[64,16,128]{2,0,1:T(8,128)S(1)})) conditional(s32[]{:T(128)} %convert_element_type.111, (f32[64,16]{0,1:T(8,128)S(1)}, f32[64,16]{0,1:T(8,128)S(1)}, f32[64,16,128]{2,0,1:T(8,128)S(1)}) %tuple.134, (s32[256]{0:T(256)S(1)}, s32[256]{0:T(256)S(1)}, s32[256]{0:T(256)S(1)}, ...), branch_computations={%region_9.9_spmd, %region_10.12_spmd} | conditional | flops 137023488 | bytes 5892640 | solution.py:81
  130.3 1.8 %conditional.9 = ((f32[64,16]{0,1:T(8,128)S(1)}, f32[64,16]{0,1:T(8,128)S(1)}, f32[64,16,128]{2,0,1:T(8,128)S(1)})) conditional(s32[]{:T(128)} %convert_element_type.110, (f32[64,16]{0,1:T(8,128)S(1)}, f32[64,16]{0,1:T(8,128)S(1)}, f32[64,16,128]{2,0,1:T(8,128)S(1)}) %tuple.132, (s32[256]{0:T(256)S(1)}, s32[256]{0:T(256)S(1)}, s32[256]{0:T(256)S(1)}, ...), branch_computations={%region_14.14_spmd, %region_15.17_spmd} | conditional | flops 137023488 | bytes 5892640 | solution.py:81
  132.7 1.9 %conditional.8 = ((f32[64,16]{0,1:T(8,128)S(1)}, f32[64,16]{0,1:T(8,128)S(1)}, f32[64,16,128]{2,0,1:T(8,128)S(1)})) conditional(s32[]{:T(128)} %convert_element_type.109, (f32[64,16]{0,1:T(8,128)S(1)}, f32[64,16]{0,1:T(8,128)S(1)}, f32[64,16,128]{2,0,1:T(8,128)S(1)}) %tuple.130, (s32[256]{0:T(256)S(1)}, s32[256]{0:T(256)S(1)}, s32[256]{0:T(256)S(1)}, ...), branch_computations={%region_19.19_spmd, %region_20.22_spmd} | conditional | flops 137023488 | bytes 5892640 | solution.py:81
  138.7 1.7 fusion.81
  145.2 1.9 %divide_convert_fusion = bf16[256,16,128]{2,0,1:T(8,128)(2,1)S(1)} fusion(f32[256,16,128]{2,0,1:T(8,128)} %get-tuple-element.329, f32[256,16]{0,1:T(8,128)S(1)} %get-tuple-element.330), kind=kLoop, calls=%fused_computation.104 | loop fusion | flops 1048576 | bytes 3162112 | tf_op jit(solution)/shard_map/convert_element_type | solution.py:118
  148.4 20.3 %all_to_all.16 = bf16[4,64,2048]{2,1,0:T(8,128)(2,1)S(1)} all-to-all(bf16[4,64,2048]{2,1,0:T(8,128)(2,1)S(1)} %convert_element_type.90), channel_id=1, replica_groups=mesh['srv'=8,'head'=4] {'head'}, dimensions={0} | all-to-all | bytes 2097152 | tf_op jit(solution)/shard_map/all_to_all | solution.py:143
  (250 shorter events, 68.3 us)
Async XLA Ops:
  6.5 3.6 %copy-start = (bf16[256,2048]{1,0:T(8,128)(2,1)S(1)}, bf16[256,2048]{1,0:T(8,128)(2,1)}, u32[]{:S(2)}) copy-start(bf16[256,2048]{1,0:T(8,128)(2,1)} %param.13) | copy-start | bytes 3145732
  6.5 31.9 %all-gather.2.cloned.1.call-start = ((), (), s32[]{:S(2)}) async-start(), calls=%async_computation.1 | async-start | bytes 2359296 | tf_op jit(solution)/shard_map/all_gather | solution.py:108
Sparse Core Ops, SparseCore 0:
  10.0 28.3 all-gather.1
where the time goes:
time: 178 us; the launch traced here: 177 us
  other arithmetic  42.2 us (24%)
  local copies, waits for them, and re-layouts  38 us (21%)
  loops' own time  25.9 us (15%)
  waiting for transfers between devices  25 us (14%)
  blocking collectives  20.3 us (11%)
  between operations  13.5 us (8%)
  matrix products  11.6 us (7%)
    all_gather x1, waiting for transfers between devices, attend(): kv_piece = lax.all_gather(packed_pair, 'srv', axis=0, tiled=True)  25 us
    another operation x1, loops' own time, attend(): lax.scan(one_step, running, (shards, jnp.arange(shard_count, dtype=jnp.in...  24.9 us
    all_to_all x1, blocking collectives, body(): lax.all_to_all(result, 'head', split_axis=0, concat_axis=1, tiled=True)  20.3 us
    dynamic_slice x24, local copies, waits for them, and re-layouts, attend(): lax.scan(one_step, running, (shards, jnp.arange(shard_count, dtype=jnp.in...  13.5 us
    slice x8, local copies, waits for them, and re-layouts, add_shard(): state[2][row_slice]  13.3 us
    concatenate x8, other arithmetic, add_shard(): jnp.concatenate([item[2] for item in updated], axis=0)  11.5 us
    add x16, other arithmetic, merge_shard(): run_acc * old_factor[..., None] + part_value * new_factor[..., None]  8.05 us
    reduce_sum x16, other arithmetic, merge_shard(): shard_total = jnp.sum(weights, axis=3)  6.59 us
  transfers between devices with their start and end apart: 1, of which 1 were waited for; matrix products, arithmetic and copies ran while one was open for 2% of the time, Pallas kernels for 0%

commit v1 on v0

v1 whole, which is shorter than its diff:
```python
import functools
import math

import jax
import jax.numpy as jnp
from jax import lax
from jax.experimental import pallas as pl
from jax.experimental.pallas import tpu as pltpu
from jax.sharding import PartitionSpec as P

HEAD = 128
MESH = pl.DeviceIdType.MESH


def kernel(cfg, len_ref, q_ref, kv_ref, out_ref, qraw, qrot, kvbuf, kvin, ksend, table, bias, obuf,
           lsem, qs, qr, kvs, kvr, osend, orecv):
    n_srv, n_head, G, back, tok, kvh, per, R, chunk, ndoc = cfg
    heads = kvh * per
    grp = G * tok
    n_grp = n_srv // G
    T = tok // n_head
    longest = back * grp
    W = longest + R
    width = heads * HEAD
    kw = kvh * HEAD
    nblk = grp // R
    nch = heads // chunk
    per_blk = R // T
    cw = chunk * HEAD
    srv = lax.axis_index("srv")
    z = lax.axis_index("head")
    k = srv // G
    a = srv % G

    bar = pltpu.get_barrier_semaphore()

    def greet(s, h):
        pl.semaphore_signal(bar, inc=1, device_id=(s, h), device_id_type=MESH)

    for i in range(1, n_head):
        for b in range(G):
            greet(k * G + b, (z + i) % n_head)
    for i in range(1, G):
        greet(k * G + (a + i) % G, z)
    for d in range(1, back + 1):
        @pl.when(k + d < n_grp)
        def _():
            for b in range(G):
                greet((k + d) * G + b, z)

        @pl.when(k - d >= 0)
        def _():
            for b in range(G):
                greet((k - d) * G + b, z)

    own_kv = pltpu.make_async_copy(kv_ref, kvin, lsem.at[0])
    own_kv.start()
    my_cols = pl.ds(pl.multiple_of(a * width, HEAD), width)
    own_q = pltpu.make_async_copy(q_ref.at[:, my_cols], qraw.at[a], lsem.at[1])
    own_q.start()

    for d in range(1, back + 1):
        @pl.when(k - d < 0)
        def _():
            kvbuf[:, pl.ds((back - d) * grp, grp), :] = jnp.zeros((2, grp, kw), jnp.bfloat16)

    ends = []
    total = jnp.int32(0)
    for i in range(ndoc):
        total = total + len_ref[i]
        ends.append(total)

    lane = lax.broadcasted_iota(jnp.int32, (tok, HEAD), 1)
    low = lane < HEAD // 2
    step_up = jnp.where(low, lane, lane - HEAD // 2).astype(jnp.float32) * (2.0 / HEAD)
    inverse = jnp.exp(-step_up * math.log(500000.0))

    def starts_of(rows):
        start = jnp.zeros_like(rows)
        for e in ends:
            start = jnp.where(e <= rows, e, start)
        return start

    def make_table(b):
        rows = (k * G + b) * tok + lax.broadcasted_iota(jnp.int32, (tok, HEAD), 0)
        angle = (rows - starts_of(rows)).astype(jnp.float32) * inverse
        sine = jnp.sin(angle)
        table[0] = jnp.cos(angle)
        table[1] = jnp.where(low, -sine, sine)

    def rotate(x):
        x = x.astype(jnp.float32)
        return (x * table[0] + pltpu.roll(x, HEAD // 2, 1) * table[1]).astype(jnp.bfloat16)

    make_table(a)
    own_kv.wait()
    for h in range(G * kvh):
        cols = slice(h * HEAD, (h + 1) * HEAD)
        ksend[:, cols] = rotate(kvin[0, :, cols])

    own_rows = pl.ds(pl.multiple_of(back * grp + a * tok, tok), tok)
    kv_cols = pl.ds(pl.multiple_of(a * kw, HEAD), kw)
    kvbuf[0, own_rows, :] = ksend[:, kv_cols]
    kvbuf[1, own_rows, :] = kvin[1, :, kv_cols]

    count = (n_head - 1) * G + (G - 1)
    for d in range(1, back + 1):
        count = count + G * jnp.where(k + d < n_grp, 1, 0) + G * jnp.where(k - d >= 0, 1, 0)
    pl.semaphore_wait(bar, count)

    def kv_copy(d, i, which):
        b = (a + i) % G
        cols = pl.ds(pl.multiple_of(b * kw, HEAD), kw)
        src = ksend.at[:, cols] if which == 0 else kvin.at[1, :, cols]
        rows = pl.ds(pl.multiple_of((back - d) * grp + a * tok, tok), tok)
        return pltpu.make_async_remote_copy(
            src_ref=src, dst_ref=kvbuf.at[which, rows, :],
            send_sem=kvs.at[d, i, which], recv_sem=kvr.at[d, a, which],
            device_id=((k + d) * G + b, z), device_id_type=MESH)

    def kv_wait(d, b, which):
        rows = pl.ds(pl.multiple_of((back - d) * grp + b * tok, tok), tok)
        ref = kvbuf.at[which, rows, :]
        pltpu.make_async_copy(ref, ref, kvr.at[d, b, which]).wait()

    for d in range(1, back + 1):
        @pl.when(k + d < n_grp)
        def _():
            for i in range(G):
                for which in (1, 0):
                    kv_copy(d, i, which).start()
    q_copies = []
    for i in range(1, G):
        b = (a + i) % G
        for which in (1, 0):
            kv_copy(0, i, which).start()
        cols = pl.ds(pl.multiple_of(b * width, HEAD), width)
        c = pltpu.make_async_remote_copy(
            src_ref=q_ref.at[:, cols], dst_ref=qraw.at[a],
            send_sem=qs.at[i], recv_sem=qr.at[a],
            device_id=(k * G + b, z), device_id_type=MESH)
        c.start()
        q_copies.append(c)

    def rotate_queries(b):
        for h in range(heads):
            qrot[h, pl.ds(pl.multiple_of(b * tok, tok), tok), :] = rotate(
                qraw[b, :, h * HEAD:(h + 1) * HEAD])

    own_q.wait()
    rotate_queries(a)
    for i in range(1, G):
        b = (a + i) % G
        make_table(b)
        pltpu.make_async_copy(qraw.at[b], qraw.at[b], qr.at[b]).wait()
        rotate_queries(b)

    for i in range(1, G):
        for which in range(2):
            kv_wait(0, (a + i) % G, which)
    for d in range(1, back + 1):
        @pl.when(k - d >= 0)
        def _():
            for b in range(G):
                for which in range(2):
                    kv_wait(d, b, which)

    nbm = tok // R
    zpart = z * nbm // n_head
    scale = HEAD ** -0.5 * math.log2(math.e)

    def where_of(s):
        blk = s // nch
        c = s % nch
        b = G - 1 - blk % G
        part = (zpart + 1 + blk // G) % nbm
        return blk, c, b, part

    def out_copy(s, j):
        blk, c, b, part = where_of(s)
        dest = part * per_blk + j
        col = pl.multiple_of(z * (G * width) + a * width + c * cw, HEAD)
        src = obuf.at[s, pl.ds(j * T, T), :]
        dst = out_ref.at[:, pl.ds(col, cw)]
        idx = (z * G + a) * nch + c
        remote = pltpu.make_async_remote_copy(
            src_ref=src, dst_ref=dst, send_sem=osend.at[s * per_blk + j], recv_sem=orecv.at[idx],
            device_id=(k * G + b, dest), device_id_type=MESH)
        local = pltpu.make_async_copy(src, dst, orecv.at[idx])
        mine = jnp.logical_and(b == a, dest == z)
        return mine, remote, local

    def one_step(s, carry):
        blk, c, b, part = where_of(s)
        r0 = pl.multiple_of(b * tok + part * R, R)

        @pl.when(c == 0)
        def _():
            rows = k * grp + r0 + lax.broadcasted_iota(jnp.int32, (R, HEAD), 0)
            start = starts_of(rows)
            for j in range(W // HEAD):
                t = (k - back) * grp + r0 + j * HEAD + lax.broadcasted_iota(jnp.int32, (R, HEAD), 1)
                ok = jnp.logical_and(t >= start, t <= rows)
                bias[:, j * HEAD:(j + 1) * HEAD] = jnp.where(ok, 0.0, -1e30)

        kcol = pl.ds(pl.multiple_of((c * chunk // per) * HEAD, HEAD), HEAD)
        keys = kvbuf[0, pl.ds(r0, W), kcol]
        vals = kvbuf[1, pl.ds(r0, W), kcol]
        vals = jnp.concatenate([vals, jnp.ones_like(vals)], axis=1)
        q = qrot[pl.ds(c * chunk, chunk), pl.ds(r0, R), :].reshape(chunk * R, HEAD)
        sc = lax.dot_general(q, keys, (((1,), (1,)), ((), ())), preferred_element_type=jnp.float32)
        sc = (sc.reshape(chunk, R, W) + bias[...][None]).reshape(chunk * R, W)
        top = jnp.max(sc, axis=1, keepdims=True)
        w = jnp.exp2((sc - top) * scale).astype(jnp.bfloat16)
        acc = lax.dot_general(w, vals, (((1,), (0,)), ((), ())), preferred_element_type=jnp.float32)
        o = (acc[:, :HEAD] / acc[:, HEAD:]).astype(jnp.bfloat16)
        for h in range(chunk):
            obuf[s, :, h * HEAD:(h + 1) * HEAD] = o[h * R:(h + 1) * R, :]

        for j in range(per_blk):
            mine, remote, local = out_copy(s, j)

            @pl.when(mine)
            def _():
                local.start()

            @pl.when(jnp.logical_not(mine))
            def _():
                remote.start()
        return carry

    lax.fori_loop(0, nblk * nch, one_step, 0)

    for i in range(1, G):
        for which in (1, 0):
            kv_copy(0, i, which).wait_send()
    for c in q_copies:
        c.wait_send()
    for d in range(1, back + 1):
        @pl.when(k + d < n_grp)
        def _():
            for i in range(G):
                for which in (1, 0):
                    kv_copy(d, i, which).wait_send()

    def end_send(s, carry):
        for j in range(per_blk):
            mine, remote, local = out_copy(s, j)

            @pl.when(jnp.logical_not(mine))
            def _():
                remote.wait_send()
        return carry

    lax.fori_loop(0, nblk * nch, end_send, 0)

    def end_recv(i, carry):
        col = pl.multiple_of(i * cw, HEAD)
        ref = out_ref.at[:, pl.ds(col, cw)]
        pltpu.make_async_copy(ref, ref, orecv.at[i]).wait()
        return carry

    lax.fori_loop(0, n_head * G * nch, end_recv, 0)


def solution(mesh):
    n_srv, n_head = mesh.shape["srv"], mesh.shape["head"]

    def body(queries, key_value_pair, lengths):
        tok, qw = queries.shape
        kv_all = key_value_pair.shape[2] // HEAD
        G = 2 if kv_all % 2 == 0 and n_srv % 2 == 0 else 1
        kvh = kv_all // G
        per = qw // HEAD // kv_all
        grp = G * tok
        n_grp = n_srv // G
        back = n_grp // 2
        T = tok // n_head
        R = max(tok // 2, T)
        chunk = per // 2
        ndoc = lengths.shape[0]
        heads = kvh * per
        nsteps = (grp // R) * (heads // chunk)
        W = back * grp + R
        cfg = (n_srv, n_head, G, back, tok, kvh, per, R, chunk, ndoc)
        bf = jnp.bfloat16
        dma = pltpu.SemaphoreType.DMA
        return pl.pallas_call(
            functools.partial(kernel, cfg),
            out_shape=jax.ShapeDtypeStruct((T, qw * n_head), bf),
            in_specs=[
                pl.BlockSpec(memory_space=pltpu.SMEM),
                pl.BlockSpec(memory_space=pl.ANY),
                pl.BlockSpec(memory_space=pl.ANY),
            ],
            out_specs=pl.BlockSpec(memory_space=pl.ANY),
            scratch_shapes=[
                pltpu.VMEM((G, tok, heads * HEAD), bf),
                pltpu.VMEM((heads, grp, HEAD), bf),
                pltpu.VMEM((2, (back + 1) * grp, kvh * HEAD), bf),
                pltpu.VMEM((2, tok, kv_all * HEAD), bf),
                pltpu.VMEM((tok, kv_all * HEAD), bf),
                pltpu.VMEM((2, tok, HEAD), jnp.float32),
                pltpu.VMEM((R, W), jnp.float32),
                pltpu.VMEM((nsteps, R, chunk * HEAD), bf),
                dma((2,)),
                dma((G,)),
                dma((G,)),
                dma((back + 1, G, 2)),
                dma((back + 1, G, 2)),
                dma((nsteps * (R // T),)),
                dma((n_head * G * (heads // chunk),)),
            ],
            compiler_params=pltpu.CompilerParams(collective_id=0, has_side_effects=True),
            name="attend",
        )(lengths, queries, key_value_pair)

    in_specs = (P("srv", "head"), P(None, "srv", "head"), P())
    out_specs = P(("srv", "head"), None)
    return jax.shard_map(body, mesh=mesh, in_specs=in_specs, out_specs=out_specs, check_vma=False)
```

time: 178 us -> 44.7 us (0.25)
  the two profiles are of different devices: /device:TPU:6 before, /device:TPU:4 now
where the time goes in v1:
time: 44.7 us; the launch traced here: 44.4 us
  Pallas kernels  42.1 us (94%)
  local copies, waits for them, and re-layouts  2.26 us (5%)
    pallas_call x1, Pallas kernels, body(): pl.pallas_call(functools.partial(kernel, cfg), out_shape=jax.ShapeDtypeSt...  42.1 us
    unnamed x1, local copies, waits for them, and re-layouts  2.26 us

profile of v1, /device:TPU:4, one launch (start us, length us, event | category | flops | bytes accessed | tf_op | source)
XLA Modules:
  0.0 44.4 jit_solution(2357853586379524471)
XLA Ops:
  0.0 42.1 %attend.1 = bf16[64,8192]{1,0:T(8,128)(2,1)} custom-call(s32[8]{0:T(128)} %len_ref.1, bf16[256,2048]{1,0:T(8,128)(2,1)} %q_ref.1, bf16[2,256,256]{2,1,0:T(8,128)(2,1)} %kv_ref.1), custom_call_target="tpu_custom_call" | custom-call | tf_op jit(solution)/shard_map/attend/pallas_call | solution.py:288
  42.2 2.3 %copy.5 = bf16[64,8192]{1,0:T(8,128)(2,1)} copy(bf16[64,8192]{1,0:T(8,128)(2,1)} %attend.1) | data formatting | bytes 2097152

commit v2 on v1

--- a/solution.py
+++ b/solution.py
@@ -13,7 +13,7 @@
 
 
 def kernel(cfg, len_ref, q_ref, kv_ref, out_ref, qraw, qrot, kvbuf, kvin, ksend, table, bias, obuf,
-           lsem, qs, qr, kvs, kvr, osend, orecv):
+           lsem, qs, qr, kvs, kvr, fwd, osend, orecv):
     n_srv, n_head, G, back, tok, kvh, per, R, chunk, ndoc = cfg
     heads = kvh * per
     grp = G * tok
@@ -123,8 +123,25 @@
         ref = kvbuf.at[which, rows, :]
         pltpu.make_async_copy(ref, ref, kvr.at[d, b, which]).wait()
 
-    for d in range(1, back + 1):
-        @pl.when(k + d < n_grp)
+    relayed = jnp.logical_and(k % 2 == 1, k + 2 < n_grp)
+    relays = jnp.logical_and(k % 2 == 1, k >= 3)
+
+    def sends(d):
+        near = k + d < n_grp
+        if d == 1 and back >= 2:
+            near = jnp.logical_and(near, jnp.logical_not(relayed))
+        return near
+
+    def relay_copy(b, which):
+        src = pl.ds(pl.multiple_of((back - 2) * grp + b * tok, tok), tok)
+        dst = pl.ds(pl.multiple_of((back - 1) * grp + b * tok, tok), tok)
+        return pltpu.make_async_remote_copy(
+            src_ref=kvbuf.at[which, src, :], dst_ref=kvbuf.at[which, dst, :],
+            send_sem=fwd.at[b, which], recv_sem=kvr.at[1, b, which],
+            device_id=(srv - G, z), device_id_type=MESH)
+
+    for d in range(1, back + 1):
+        @pl.when(sends(d))
         def _():
             for i in range(G):
                 for which in (1, 0):
@@ -158,20 +175,29 @@
     for i in range(1, G):
         for which in range(2):
             kv_wait(0, (a + i) % G, which)
-    for d in range(1, back + 1):
+    order = [2, 1] + list(range(3, back + 1)) if back >= 2 else [1]
+    for d in order:
         @pl.when(k - d >= 0)
         def _():
             for b in range(G):
-                for which in range(2):
+                for which in (1, 0):
                     kv_wait(d, b, which)
+                    if d == 2:
+                        @pl.when(relays)
+                        def _():
+                            relay_copy(b, which).start()
 
     nbm = tok // R
     zpart = z * nbm // n_head
+    edge = n_head // 4
+    outer = jnp.logical_or(z < edge, z >= n_head - edge)
     scale = HEAD ** -0.5 * math.log2(math.e)
 
     def where_of(s):
         blk = s // nch
         c = s % nch
+        late = jnp.where(blk == 0, 0, jnp.where(blk == nblk - 1, 1, blk + 1))
+        blk = jnp.where(outer, late, blk)
         b = G - 1 - blk % G
         part = (zpart + 1 + blk // G) % nbm
         return blk, c, b, part
@@ -237,11 +263,17 @@
     for c in q_copies:
         c.wait_send()
     for d in range(1, back + 1):
-        @pl.when(k + d < n_grp)
+        @pl.when(sends(d))
         def _():
             for i in range(G):
                 for which in (1, 0):
                     kv_copy(d, i, which).wait_send()
+    if back >= 2:
+        @pl.when(relays)
+        def _():
+            for b in range(G):
+                for which in (1, 0):
+                    relay_copy(b, which).wait_send()
 
     def end_send(s, carry):
         for j in range(per_blk):
@@ -308,6 +340,7 @@
                 dma((G,)),
                 dma((back + 1, G, 2)),
                 dma((back + 1, G, 2)),
+                dma((G, 2)),
                 dma((nsteps * (R // T),)),
                 dma((n_head * G * (heads // chunk),)),
             ],

time: 44.7 us -> 44.4 us (level)
  no operation moved by 1% of the time
where the time goes in v2:
time: 44.4 us; the launch traced here: 44.2 us
  Pallas kernels  41.9 us (94%)
  local copies, waits for them, and re-layouts  2.26 us (5%)
    pallas_call x1, Pallas kernels, body(): pl.pallas_call(functools.partial(kernel, cfg), out_shape=jax.ShapeDtypeSt...  41.9 us
    unnamed x1, local copies, waits for them, and re-layouts  2.26 us

profile of v2, /device:TPU:4, one launch (start us, length us, event | category | flops | bytes accessed | tf_op | source)
XLA Modules:
  0.0 44.2 jit_solution(7890503049098991811)
XLA Ops:
  0.0 41.9 %attend.1 = bf16[64,8192]{1,0:T(8,128)(2,1)} custom-call(s32[8]{0:T(128)} %len_ref.1, bf16[256,2048]{1,0:T(8,128)(2,1)} %q_ref.1, bf16[2,256,256]{2,1,0:T(8,128)(2,1)} %kv_ref.1), custom_call_target="tpu_custom_call" | custom-call | tf_op jit(solution)/shard_map/attend/pallas_call | solution.py:320
  42.0 2.3 %copy.5 = bf16[64,8192]{1,0:T(8,128)(2,1)} copy(bf16[64,8192]{1,0:T(8,128)(2,1)} %attend.1) | data formatting | bytes 2097152

commit v3 on v2

--- a/solution.py
+++ b/solution.py
@@ -123,7 +123,7 @@
         ref = kvbuf.at[which, rows, :]
         pltpu.make_async_copy(ref, ref, kvr.at[d, b, which]).wait()
 
-    relayed = jnp.logical_and(k % 2 == 1, k + 2 < n_grp)
+    relayed = jnp.logical_and(jnp.logical_and(k % 2 == 1, k + 2 < n_grp), a == G - 1)
     relays = jnp.logical_and(k % 2 == 1, k >= 3)
 
     def sends(d):
@@ -140,16 +140,19 @@
             send_sem=fwd.at[b, which], recv_sem=kvr.at[1, b, which],
             device_id=(srv - G, z), device_id_type=MESH)
 
-    for d in range(1, back + 1):
-        @pl.when(sends(d))
+    def start_kv(d, when):
+        @pl.when(jnp.logical_and(sends(d), when))
         def _():
             for i in range(G):
-                for which in (1, 0):
+                for which in range(2):
                     kv_copy(d, i, which).start()
+
+    for d in range(1, back + 1):
+        start_kv(d, a == G - 1 if d == back else True)
     q_copies = []
     for i in range(1, G):
         b = (a + i) % G
-        for which in (1, 0):
+        for which in range(2):
             kv_copy(0, i, which).start()
         cols = pl.ds(pl.multiple_of(b * width, HEAD), width)
         c = pltpu.make_async_remote_copy(
@@ -166,26 +169,41 @@
 
     own_q.wait()
     rotate_queries(a)
+    start_kv(back, a < G - 1)
     for i in range(1, G):
         b = (a + i) % G
         make_table(b)
         pltpu.make_async_copy(qraw.at[b], qraw.at[b], qr.at[b]).wait()
         rotate_queries(b)
 
-    for i in range(1, G):
-        for which in range(2):
+    if back >= 2:
+        @pl.when(k >= 2)
+        def _():
+            for which in range(2):
+                kv_wait(2, G - 1, which)
+
+                @pl.when(relays)
+                def _():
+                    relay_copy(G - 1, which).start()
+
+    def wait_early(which):
+        for i in range(1, G):
             kv_wait(0, (a + i) % G, which)
-    order = [2, 1] + list(range(3, back + 1)) if back >= 2 else [1]
-    for d in order:
-        @pl.when(k - d >= 0)
-        def _():
-            for b in range(G):
-                for which in (1, 0):
-                    kv_wait(d, b, which)
-                    if d == 2:
-                        @pl.when(relays)
-                        def _():
-                            relay_copy(b, which).start()
+        for d in range(1, back + 1):
+            @pl.when(k - d >= 0)
+            def _():
+                for b in range(G - 1 if d == back else 0, G):
+                    if (d, b) != (2, G - 1):
+                        kv_wait(d, b, which)
+
+    def wait_late():
+        @pl.when(k - back >= 0)
+        def _():
+            for b in range(G - 1):
+                for which in range(2):
+                    kv_wait(back, b, which)
+
+    wait_early(0)
 
     nbm = tok // R
     zpart = z * nbm // n_head
@@ -220,6 +238,10 @@
         blk, c, b, part = where_of(s)
         r0 = pl.multiple_of(b * tok + part * R, R)
 
+        @pl.when(s == nch)
+        def _():
+            wait_late()
+
         @pl.when(c == 0)
         def _():
             rows = k * grp + r0 + lax.broadcasted_iota(jnp.int32, (R, HEAD), 0)
@@ -231,13 +253,18 @@
 
         kcol = pl.ds(pl.multiple_of((c * chunk // per) * HEAD, HEAD), HEAD)
         keys = kvbuf[0, pl.ds(r0, W), kcol]
-        vals = kvbuf[1, pl.ds(r0, W), kcol]
-        vals = jnp.concatenate([vals, jnp.ones_like(vals)], axis=1)
         q = qrot[pl.ds(c * chunk, chunk), pl.ds(r0, R), :].reshape(chunk * R, HEAD)
         sc = lax.dot_general(q, keys, (((1,), (1,)), ((), ())), preferred_element_type=jnp.float32)
         sc = (sc.reshape(chunk, R, W) + bias[...][None]).reshape(chunk * R, W)
         top = jnp.max(sc, axis=1, keepdims=True)
         w = jnp.exp2((sc - top) * scale).astype(jnp.bfloat16)
+
+        @pl.when(s == 0)
+        def _():
+            wait_early(1)
+
+        vals = kvbuf[1, pl.ds(r0, W), kcol]
+        vals = jnp.concatenate([vals, jnp.ones_like(vals)], axis=1)
         acc = lax.dot_general(w, vals, (((1,), (0,)), ((), ())), preferred_element_type=jnp.float32)
         o = (acc[:, :HEAD] / acc[:, HEAD:]).astype(jnp.bfloat16)
         for h in range(chunk):
@@ -271,9 +298,8 @@
     if back >= 2:
         @pl.when(relays)
         def _():
-            for b in range(G):
-                for which in (1, 0):
-                    relay_copy(b, which).wait_send()
+            for which in range(2):
+                relay_copy(G - 1, which).wait_send()
 
     def end_send(s, carry):
         for j in range(per_blk):

time: 44.4 us -> 39.2 us (0.88)
  Pallas kernels: 41.9 us -> 36.8 us
    pallas_call x1, Pallas kernels: 41.9 us -> 36.8 us  [body(): pl.pallas_call(functools.partial(kernel, cfg), out_shape=jax.ShapeDtypeSt...]
where the time goes in v3:
time: 39.2 us; the launch traced here: 39 us
  Pallas kernels  36.8 us (94%)
  local copies, waits for them, and re-layouts  2.26 us (6%)
    pallas_call x1, Pallas kernels, body(): pl.pallas_call(functools.partial(kernel, cfg), out_shape=jax.ShapeDtypeSt...  36.8 us
    unnamed x1, local copies, waits for them, and re-layouts  2.26 us

profile of v3, /device:TPU:4, one launch (start us, length us, event | category | flops | bytes accessed | tf_op | source)
XLA Modules:
  0.0 39.0 jit_solution(126335398009114444)
XLA Ops:
  0.0 36.8 %attend.1 = bf16[64,8192]{1,0:T(8,128)(2,1)} custom-call(s32[8]{0:T(128)} %len_ref.1, bf16[256,2048]{1,0:T(8,128)(2,1)} %q_ref.1, bf16[2,256,256]{2,1,0:T(8,128)(2,1)} %kv_ref.1), custom_call_target="tpu_custom_call" | custom-call | tf_op jit(solution)/shard_map/attend/pallas_call | solution.py:346
  36.8 2.3 %copy.5 = bf16[64,8192]{1,0:T(8,128)(2,1)} copy(bf16[64,8192]{1,0:T(8,128)(2,1)} %attend.1) | data formatting | bytes 2097152

commit v4 on v3

--- a/solution.py
+++ b/solution.py
@@ -345,7 +345,7 @@
         dma = pltpu.SemaphoreType.DMA
         return pl.pallas_call(
             functools.partial(kernel, cfg),
-            out_shape=jax.ShapeDtypeStruct((T, qw * n_head), bf),
+            out_shape=pltpu.VMEM((T, qw * n_head), bf),
             in_specs=[
                 pl.BlockSpec(memory_space=pltpu.SMEM),
                 pl.BlockSpec(memory_space=pl.ANY),

time: 39.2 us -> 37.8 us (0.964)
  local copies, waits for them, and re-layouts: 2.26 us -> 0.97 us
    unnamed x1, local copies, waits for them, and re-layouts: 2.26 us -> 0.97 us
where the time goes in v4:
time: 37.8 us; the launch traced here: 37.6 us
  Pallas kernels  36.6 us (97%)
  local copies, waits for them, and re-layouts  0.97 us (3%)
    pallas_call x1, Pallas kernels, body(): pl.pallas_call(functools.partial(kernel, cfg), out_shape=pltpu.VMEM((T, q...  36.6 us
    unnamed x1, local copies, waits for them, and re-layouts  0.97 us

profile of v4, /device:TPU:4, one launch (start us, length us, event | category | flops | bytes accessed | tf_op | source)
XLA Modules:
  0.0 37.6 jit_solution(7458717977197659584)
XLA Ops:
  0.0 36.6 %attend.1 = bf16[64,8192]{1,0:T(8,128)(2,1)S(1)} custom-call(s32[8]{0:T(128)} %len_ref.1, bf16[256,2048]{1,0:T(8,128)(2,1)} %q_ref.1, bf16[2,256,256]{2,1,0:T(8,128)(2,1)} %kv_ref.1), custom_call_target="tpu_custom_call" | custom-call | tf_op jit(solution)/shard_map/attend/pallas_call | solution.py:346
  36.7 1.0 %copy.5 = bf16[64,8192]{1,0:T(8,128)(2,1)} copy(bf16[64,8192]{1,0:T(8,128)(2,1)S(1)} %attend.1) | data formatting | bytes 2097152

commit v5 on v4

--- a/solution.py
+++ b/solution.py
@@ -143,9 +143,9 @@
     def start_kv(d, when):
         @pl.when(jnp.logical_and(sends(d), when))
         def _():
-            for i in range(G):
-                for which in range(2):
-                    kv_copy(d, i, which).start()
+            pairs = [(i, which) for which in range(2) for i in range(G)]
+            for i, which in pairs if d == 1 else sorted(pairs):
+                kv_copy(d, i, which).start()
 
     for d in range(1, back + 1):
         start_kv(d, a == G - 1 if d == back else True)
@@ -179,16 +179,21 @@
     if back >= 2:
         @pl.when(k >= 2)
         def _():
-            for which in range(2):
-                kv_wait(2, G - 1, which)
-
-                @pl.when(relays)
-                def _():
-                    relay_copy(G - 1, which).start()
+            kv_wait(2, G - 1, 0)
+
+            @pl.when(relays)
+            def _():
+                relay_copy(G - 1, 0).start()
+                kv_wait(2, G - 1, 1)
+                relay_copy(G - 1, 1).start()
 
     def wait_early(which):
         for i in range(1, G):
             kv_wait(0, (a + i) % G, which)
+        if which == 1 and back >= 2:
+            @pl.when(jnp.logical_and(k >= 2, jnp.logical_not(relays)))
+            def _():
+                kv_wait(2, G - 1, 1)
         for d in range(1, back + 1):
             @pl.when(k - d >= 0)
             def _():

time: 37.8 us -> 37 us (0.979)
  Pallas kernels: 36.6 us -> 35.9 us
    pallas_call x1, Pallas kernels: 36.6 us -> 35.9 us  [body(): pl.pallas_call(functools.partial(kernel, cfg), out_shape=pltpu.VMEM((T, q...]
where the time goes in v5:
time: 37 us; the launch traced here: 36.8 us
  Pallas kernels  35.9 us (97%)
  local copies, waits for them, and re-layouts  0.97 us (3%)
    pallas_call x1, Pallas kernels, body(): pl.pallas_call(functools.partial(kernel, cfg), out_shape=pltpu.VMEM((T, q...  35.9 us
    unnamed x1, local copies, waits for them, and re-layouts  0.97 us

profile of v5, /device:TPU:4, one launch (start us, length us, event | category | flops | bytes accessed | tf_op | source)
XLA Modules:
  0.0 36.8 jit_solution(2472418934156758766)
XLA Ops:
  0.0 35.9 %attend.1 = bf16[64,8192]{1,0:T(8,128)(2,1)S(1)} custom-call(s32[8]{0:T(128)} %len_ref.1, bf16[256,2048]{1,0:T(8,128)(2,1)} %q_ref.1, bf16[2,256,256]{2,1,0:T(8,128)(2,1)} %kv_ref.1), custom_call_target="tpu_custom_call" | custom-call | tf_op jit(solution)/shard_map/attend/pallas_call | solution.py:351
  35.9 1.0 %copy.5 = bf16[64,8192]{1,0:T(8,128)(2,1)} copy(bf16[64,8192]{1,0:T(8,128)(2,1)S(1)} %attend.1) | data formatting | bytes 2097152
